TPU v7x, 32 devices: a whole 2x2x4 slice. The times are simulated.
32 devices in a mesh: tm: 8 (over y, x, core), lat: 4 (over z).
Axes of the slice: x: 2, y: 2, z: 4, core: 2. Of those that a mesh axis runs over, the one named last changes fastest.
Arguments:
- incr_static: float32 [8, 32, 192, 128], P('tm', 'lat'), may hold values from -6 to 6
- ens_pert: bfloat16 [8, 8, 32, 192, 128], P(None, 'tm', 'lat'), may hold values from -0.59765625 to 0.59765625
- ens_weight: float32 [8, 4, 1024], P(None, 'lat', 'tm'), may hold values from -6 to 6
- column_map: int32 [32, 192], P('lat'), may hold values from 0 to 1023
- sub_steps: int32 [8], P('tm'), may hold values from 1 to 4, 24 in all
- diffusion: bfloat16 [8, 32, 192, 128], P('tm', 'lat'), may hold values from 0.0099487305 to 0.23925781
- mode_in: bfloat16 [4, 128, 128], replicated, may hold values from -0.5 to 0.5
- mode_out: bfloat16 [4, 128, 128], replicated, may hold values from -0.25 to 0.25
- model_precision: bfloat16 [8, 32, 192, 128], P('tm', 'lat'), may hold values from 0.099609375 to 1
- obs_precision: bfloat16 [8, 32, 192, 128], P('tm', 'lat'), may hold values from 0.099609375 to 1
- innovation: bfloat16 [8, 32, 192, 128], P('tm', 'lat'), may hold values from -6 to 6
Outputs:
- grad_static: float32 [8, 32, 192, 128], P('tm', 'lat')
- grad_weight: float32 [8, 4, 1024], P(None, 'lat', 'tm')
Inputs may be any that keep to these rules, and one draw needn't show every extreme that they name: `column_map`: each cell names one of the 1024 weight columns of its own latitude slab. `sub_steps`: the subwindows' step counts add up to 24.
All inputs are finite; a program needn't handle non-finite values. No bound on the sum of `sub_steps` on one device may be relied on, other than what follows from the above.
Results may differ from a plain program's by a relative error of at most 0.0065.
Values may be sent and summed in bfloat16 or wider, within the bound.
A program may use at most 64 MiB of HBM per device.

v0:
```python
import jax
import jax.numpy as jnp
from jax import lax
from jax.experimental import pallas as pl
from jax.experimental.pallas import tpu as pltpu
from jax.sharding import PartitionSpec as P

MESH = pl.DeviceIdType.MESH
F32, BF16 = jnp.float32, jnp.bfloat16
GROUP = 2
LAST = (((1,), (1,)), ((), ()))


def halves(x):
    high = x.astype(BF16)
    low = (x - high.astype(F32)).astype(BF16)
    return jnp.concatenate([high, low], axis=0)


def kernel(
    tm_count, lat_count, sizes,
    steps_ref, incr_h, pert_h, weight_h, cmap_h, diff_h, min_h, mout_h, prec_h, obs_h, innov_h,
    grad_h, gw_ref,
    incr, pert, gathered, cmap, cpad, diff, m_in, m_out, prec, obs, innov,
    onehot, start, start_bf, a_buf, b_buf, state_halo, start_next, prec_next,
    end_bf, end_prev, u_buf, seed_bf, seed_halo, c_buf, w_buf, mw_t, contrib, grad,
    term_send, term_recv, local_sem, send_sem, recv_sem, ag_send, ag_recv, rs_send, rs_recv,
):
    H, R, LON, LEV, MEM, CW = sizes
    C = CW * tm_count
    PAD = cpad.shape[1]
    me_t, me_l = lax.axis_index("tm"), lax.axis_index("lat")
    has_up, has_down = me_l > 0, me_l < lat_count - 1
    has_prev, has_next = me_t > 0, me_t < tm_count - 1

    def local(i, src, dst):
        return pltpu.make_async_copy(src, dst, local_sem.at[i])

    def remote(i, src, dst, tm, lat):
        return pltpu.make_async_remote_copy(
            src_ref=src, dst_ref=dst, send_sem=send_sem.at[i], recv_sem=recv_sem.at[i],
            device_id=(tm, lat), device_id_type=MESH,
        )

    loads = dict(
        weight=local(0, weight_h, gathered.at[me_t]),
        cmap=local(1, cmap_h, cmap),
        pert=local(2, pert_h.at[:, 0], pert),
        incr=local(3, incr_h.at[0], incr),
        diff=local(4, diff_h.at[0], diff.at[pl.ds(H, R)]),
        m_in=local(5, min_h, m_in),
        m_out=local(6, mout_h, m_out),
        prec=local(7, prec_h.at[0], prec),
        obs=local(8, obs_h.at[0], obs),
        innov=local(9, innov_h.at[0], innov),
    )
    for copy in loads.values():
        copy.start()

    barrier = pltpu.get_barrier_semaphore()
    for d in range(1, tm_count):
        pl.semaphore_signal(barrier, inc=1, device_id=(lax.rem(me_t + d, tm_count), me_l), device_id_type=MESH)

    @pl.when(has_up)
    def _():
        pl.semaphore_signal(barrier, inc=1, device_id=(me_t, me_l - 1), device_id_type=MESH)

    @pl.when(has_down)
    def _():
        pl.semaphore_signal(barrier, inc=1, device_id=(me_t, me_l + 1), device_id_type=MESH)

    @pl.when(jnp.logical_not(has_up))
    def _():
        diff[0:H] = jnp.zeros((H, LON, LEV), BF16)
        state_halo[0] = jnp.zeros((H, LON, LEV), BF16)
        seed_halo[0] = jnp.zeros((H, LON, LEV), BF16)

    @pl.when(jnp.logical_not(has_down))
    def _():
        diff[H + R:2 * H + R] = jnp.zeros((H, LON, LEV), BF16)
        state_halo[1] = jnp.zeros((H, LON, LEV), BF16)
        seed_halo[1] = jnp.zeros((H, LON, LEV), BF16)

    @pl.when(jnp.logical_not(has_prev))
    def _():
        end_prev[...] = jnp.zeros((R, LON, LEV), BF16)

    @pl.when(jnp.logical_not(has_next))
    def _():
        start_next[...] = jnp.zeros((R, LON, LEV), BF16)
        prec_next[...] = jnp.zeros((R, LON, LEV), BF16)

    loads["weight"].wait()
    pl.semaphore_wait(barrier, tm_count - 1 + has_up.astype(jnp.int32) + has_down.astype(jnp.int32))

    def spread(d):
        peer = lax.rem(me_t + d, tm_count)
        return pltpu.make_async_remote_copy(
            src_ref=gathered.at[me_t], dst_ref=gathered.at[me_t], send_sem=ag_send.at[d],
            recv_sem=ag_recv.at[d], device_id=(peer, me_l), device_id_type=MESH,
        )

    def term(d):
        peer = lax.rem(me_t + d, tm_count)
        return pltpu.make_async_remote_copy(
            src_ref=term_send.at[peer], dst_ref=term_recv.at[me_t], send_sem=rs_send.at[d],
            recv_sem=rs_recv.at[d], device_id=(peer, me_l), device_id_type=MESH,
        )

    for d in range(1, tm_count):
        spread(d).start()

    diff_up = remote(0, diff_h.at[0, pl.ds(0, H)], diff.at[pl.ds(H + R, H)], me_t, me_l - 1)
    diff_down = remote(1, diff_h.at[0, pl.ds(R - H, H)], diff.at[pl.ds(0, H)], me_t, me_l + 1)
    prec_back = remote(2, prec_h.at[0], prec_next, me_t - 1, me_l)
    start_back = remote(3, start_bf, start_next, me_t - 1, me_l)
    end_on = remote(4, end_bf, end_prev, me_t + 1, me_l)
    Q = GROUP if H % GROUP == 0 else 1
    parts = H // Q

    def edge_copies(base, field, halo):
        ups, downs = [], []
        for c in range(parts):
            first = c * Q
            ups.append(remote(base + c, field.at[pl.ds(first, Q)], halo.at[1, pl.ds(first, Q)], me_t, me_l - 1))
            first = H - (c + 1) * Q
            downs.append(remote(
                base + parts + c, field.at[pl.ds(R - H + first, Q)], halo.at[0, pl.ds(first, Q)], me_t, me_l + 1
            ))
        return ups, downs

    state_up, state_down = edge_copies(5, start_bf, state_halo)
    seed_up, seed_down = edge_copies(5 + 2 * parts, seed_bf, seed_halo)

    def go(copy, there):
        @pl.when(there)
        def _():
            copy.start()

    def sent(copy, there):
        @pl.when(there)
        def _():
            copy.wait_send()

    def got(copy, there):
        @pl.when(there)
        def _():
            copy.wait_recv()

    go(diff_up, has_up)
    go(diff_down, has_down)
    go(prec_back, has_prev)

    loads["cmap"].wait()
    cpad[...] = jnp.full(cpad.shape, -1, jnp.int32)
    cpad[:, 0:LON] = cmap[...]
    contrib[...] = jnp.zeros(contrib.shape, F32)
    LANES = PAD
    CH = 128 if C % 128 == 0 else C

    def indicate(chunk, carry):
        base = pl.multiple_of(chunk * CH, CH)
        rows = lax.broadcasted_iota(jnp.int32, (CH, LANES), 0) + base
        for i in range(R):
            hit = jnp.where(rows == cpad[i:i + 1, :], 1.0, 0.0).astype(BF16)
            onehot[pl.ds(base, CH), i * LANES:(i + 1) * LANES] = hit
        return carry

    lax.fori_loop(0, C // CH, indicate, 0)

    for d in range(1, tm_count):
        spread(d).wait_recv()
    weights = jnp.concatenate([gathered[p] for p in range(tm_count)], axis=1)
    picked = jnp.dot(halves(weights), onehot[...], preferred_element_type=F32)
    mw_t[...] = jnp.transpose(picked[0:MEM] + picked[MEM:2 * MEM])

    loads["pert"].wait()
    loads["incr"].wait()

    def begin(first, count):
        for i in range(first, first + count):
            cols = mw_t[i * LANES:i * LANES + LON, :]
            row = incr[i]
            for k in range(MEM):
                row = row + pert[k, i].astype(F32) * cols[:, k:k + 1]
            start[i] = row
            a_buf[i + H] = row
            start_bf[i] = row.astype(BF16)

    def blocks(row, first, count):
        done = 0
        while done < count:
            size = min(GROUP, count - done)
            row(first + done, size)
            done += size

    def from_edges(row, ups, downs):
        for c in range(parts):
            row(c * Q, Q)
            go(ups[c], has_up)
            row(R - (c + 1) * Q, Q)
            go(downs[c], has_down)
        blocks(row, H, R - 2 * H)

    from_edges(begin, state_up, state_down)
    go(start_back, has_prev)

    step_count = steps_ref[0]
    loads["diff"].wait()
    loads["m_in"].wait()
    loads["m_out"].wait()

    def laplacian(field, r, count):
        here = field[pl.ds(r, count)]
        sides = pltpu.roll(here, 1, 1) + pltpu.roll(here, LON - 1, 1)
        return here, field[pl.ds(r - 1, count)] + field[pl.ds(r + 1, count)] + sides - 4.0 * here

    def forward_rows(n, src, dst, r, count):
        here, lap = laplacian(src, r, count)
        smoothed = here + diff[pl.ds(r, count)].astype(F32) * lap
        flat = smoothed.astype(BF16).reshape(count * LON, LEV)
        modes = jnp.dot(flat, m_in[n], preferred_element_type=F32).astype(BF16)
        moved = jnp.dot(modes, m_out[n], preferred_element_type=F32)
        advanced = smoothed + moved.reshape(count, LON, LEV)
        result = jnp.where(n < step_count, advanced, here)
        dst[pl.ds(r, count)] = result
        return result

    def buffers(n):
        return (a_buf, b_buf) if n % 2 == 0 else (b_buf, a_buf)

    def forward_inner(n):
        src, dst = buffers(n)
        blocks(lambda r, c: forward_rows(n, src, dst, r, c), H + n + 1, R - 2 * n - 2)

    def forward_edges(n):
        src, dst = buffers(n)
        blocks(lambda r, c: forward_rows(n, src, dst, r, c), n + 1, H)
        blocks(lambda r, c: forward_rows(n, src, dst, r, c), H + R - n - 1, H)

    for n in range(H - 1):
        forward_inner(n)
    got(diff_up, has_down)
    got(diff_down, has_up)
    for copy in state_up:
        got(copy, has_down)
    for copy in state_down:
        got(copy, has_up)

    def widen(i, carry):
        a_buf[i] = state_halo[0, i].astype(F32)
        a_buf[i + H + R] = state_halo[1, i].astype(F32)
        return carry

    lax.fori_loop(0, H, widen, 0)
    for n in range(H - 1):
        forward_edges(n)
    loads["obs"].wait()
    loads["innov"].wait()
    got(prec_back, has_next)
    got(start_back, has_next)
    src, dst = buffers(H - 1)

    def finish(i, count):
        rows = pl.ds(i, count)
        end = forward_rows(H - 1, src, dst, i + H, count)
        misfit = obs[rows].astype(F32) * (end - innov[rows].astype(F32))
        seed = misfit - prec_next[rows].astype(F32) * (start_next[rows].astype(F32) - end)
        end_bf[rows] = end.astype(BF16)
        u_buf[pl.ds(i + H, count)] = seed
        seed_bf[rows] = seed.astype(BF16)

    from_edges(finish, seed_up, seed_down)
    go(end_on, has_next)

    def couple(m, r, count):
        n = H - 1 - m
        rows = pl.ds(r, count)
        here = u_buf[rows]
        flat = here.astype(BF16).reshape(count * LON, LEV)
        modes = lax.dot_general(flat, m_out[n], LAST, preferred_element_type=F32).astype(BF16)
        moved = lax.dot_general(modes, m_in[n], LAST, preferred_element_type=F32)
        coupled = here + moved.reshape(count, LON, LEV)
        c_buf[m % 2, rows] = coupled
        w_buf[m % 2, rows] = diff[rows].astype(F32) * coupled

    def settle(m, r, count):
        rows = pl.ds(r, count)
        _, lap = laplacian(w_buf.at[m % 2], r, count)
        u_buf[rows] = jnp.where(H - 1 - m < step_count, c_buf[m % 2, rows] + lap, u_buf[rows])

    for m in range(H):
        blocks(lambda r, c: couple(m, r, c), H + m, R - 2 * m)
        blocks(lambda r, c: settle(m, r, c), H + m + 1, R - 2 * m - 2)
    for copy in seed_up:
        got(copy, has_down)
    for copy in seed_down:
        got(copy, has_up)

    def widen_seed(i, carry):
        u_buf[i] = seed_halo[0, i].astype(F32)
        u_buf[i + H + R] = seed_halo[1, i].astype(F32)
        return carry

    lax.fori_loop(0, H, widen_seed, 0)
    for m in range(H):
        blocks(lambda r, c: couple(m, r, c), m, H)
        blocks(lambda r, c: couple(m, r, c), H + R - m, H)
        blocks(lambda r, c: settle(m, r, c), m + 1, H)
        blocks(lambda r, c: settle(m, r, c), H + R - m - 1, H)

    got(end_on, has_prev)
    loads["prec"].wait()
    lane = lax.broadcasted_iota(jnp.int32, (MEM, MEM * LEV), 1)
    member = lax.broadcasted_iota(jnp.int32, (MEM, MEM * LEV), 0) * LEV
    own = jnp.where((lane >= member) & (lane < member + LEV), 1.0, 0.0).astype(BF16)

    for i in range(R):
        jump = prec[i].astype(F32) * (start[i] - end_prev[i].astype(F32))
        total = jump + u_buf[i + H]
        grad[i] = total
        terms = jnp.concatenate([(pert[k, i].astype(F32) * total).astype(BF16) for k in range(MEM)], axis=1)
        contrib[:, i * LANES:i * LANES + LON] = lax.dot_general(own, terms, LAST, preferred_element_type=F32)

    store = local(10, grad, grad_h.at[0])
    store.start()
    sums = lax.dot_general(halves(contrib[...]), onehot[...], LAST, preferred_element_type=F32)
    sums = sums[0:MEM] + sums[MEM:2 * MEM]
    for p in range(tm_count):
        term_send[p] = sums[:, p * CW:(p + 1) * CW]
    for d in range(1, tm_count):
        term(d).start()
    result = gathered[me_t] + term_send[me_t]
    for d in range(1, tm_count):
        term(d).wait_recv()
    for d in range(1, tm_count):
        result = result + term_recv[lax.rem(me_t + d, tm_count)]
    gw_ref[...] = result

    for d in range(1, tm_count):
        spread(d).wait_send()
        term(d).wait_send()
    for copy in [diff_up] + state_up + seed_up:
        sent(copy, has_up)
    for copy in [diff_down] + state_down + seed_down:
        sent(copy, has_down)
    sent(prec_back, has_prev)
    sent(start_back, has_prev)
    sent(end_on, has_next)
    store.wait()


def deliver(grad_h, owned_h, out_h, gw_ref, buf, small, sem_in, sem_out, sem_small):
    R = buf.shape[0]
    pieces = 4 if R % 4 == 0 else 1
    size = R // pieces
    ins, outs = [], []
    for i in range(pieces):
        rows = pl.ds(i * size, size)
        ins.append(pltpu.make_async_copy(grad_h.at[0, rows], buf.at[rows], sem_in.at[i]))
        outs.append(pltpu.make_async_copy(buf.at[rows], out_h.at[0, rows], sem_out.at[i]))
    fetch = pltpu.make_async_copy(owned_h, small, sem_small.at[0])
    for copy in ins:
        copy.start()
    fetch.start()
    for arrive, leave in zip(ins, outs):
        arrive.wait()
        leave.start()
    fetch.wait()
    gw_ref[:, 0, :] = small[...]
    for copy in outs:
        copy.wait()


def solution(mesh):
    tm_count, lat_count = mesh.shape["tm"], mesh.shape["lat"]

    def body(incr, pert, weight, cmap, steps, diffusion, m_in, m_out, prec, obs, innov):
        _, R, LON, LEV = incr.shape
        MEM, _, CW = weight.shape
        H = m_in.shape[0]
        PAD = -(-LON // 128) * 128
        field = lambda rows, kind: pltpu.VMEM((rows, LON, LEV), kind)
        wide = 2 * H + R
        scratch = [
            field(R, F32),
            pltpu.VMEM((MEM, R, LON, LEV), BF16),
            pltpu.VMEM((tm_count, MEM, CW), F32),
            pltpu.VMEM((R, LON), jnp.int32),
            pltpu.VMEM((R, PAD), jnp.int32),
            field(wide, BF16),
            pltpu.VMEM(m_in.shape, BF16),
            pltpu.VMEM(m_out.shape, BF16),
            field(R, BF16), field(R, BF16), field(R, BF16),
            pltpu.VMEM((CW * tm_count, R * PAD), BF16),
            field(R, F32), field(R, BF16), field(wide, F32), field(wide, F32),
            pltpu.VMEM((2, H, LON, LEV), BF16),
            field(R, BF16), field(R, BF16), field(R, BF16), field(R, BF16),
            field(wide, F32), field(R, BF16),
            pltpu.VMEM((2, H, LON, LEV), BF16),
            pltpu.VMEM((2, wide, LON, LEV), F32),
            pltpu.VMEM((2, wide, LON, LEV), F32),
            pltpu.VMEM((R * PAD, MEM), F32),
            pltpu.VMEM((MEM, R * PAD), F32),
            field(R, F32),
            pltpu.VMEM((tm_count, MEM, CW), F32),
            pltpu.VMEM((tm_count, MEM, CW), F32),
            pltpu.SemaphoreType.DMA((11,)),
            pltpu.SemaphoreType.DMA((5 + 4 * H,)),
            pltpu.SemaphoreType.DMA((5 + 4 * H,)),
        ] + [pltpu.SemaphoreType.DMA((tm_count,))] * 4

        def run(*refs):
            kernel(tm_count, lat_count, (H, R, LON, LEV, MEM, CW), *refs)

        grad, owned = pl.pallas_call(
            run,
            out_shape=(
                jax.ShapeDtypeStruct(incr.shape, F32),
                jax.ShapeDtypeStruct((MEM, CW), F32),
            ),
            in_specs=[pl.BlockSpec(memory_space=pltpu.SMEM)] + [pl.BlockSpec(memory_space=pl.ANY)] * 10,
            out_specs=(pl.BlockSpec(memory_space=pl.ANY), pl.BlockSpec(memory_space=pltpu.VMEM)),
            scratch_shapes=scratch,
            compiler_params=pltpu.CompilerParams(
                collective_id=0, has_side_effects=True, vmem_limit_bytes=60 * 1024 * 1024
            ),
        )(steps, incr, pert, weight[:, 0], cmap, diffusion, m_in, m_out, prec, obs, innov)
        return pl.pallas_call(
            deliver,
            out_shape=(
                jax.ShapeDtypeStruct(incr.shape, F32),
                jax.ShapeDtypeStruct((MEM, 1, CW), F32),
            ),
            in_specs=[pl.BlockSpec(memory_space=pl.ANY)] * 2,
            out_specs=(pl.BlockSpec(memory_space=pl.ANY), pl.BlockSpec(memory_space=pltpu.VMEM)),
            scratch_shapes=[
                field(R, F32),
                pltpu.VMEM((MEM, CW), F32),
                pltpu.SemaphoreType.DMA((4,)),
                pltpu.SemaphoreType.DMA((4,)),
                pltpu.SemaphoreType.DMA((1,)),
            ],
        )(grad, owned)

    return jax.shard_map(
        body,
        mesh=mesh,
        in_specs=(
            P("tm", "lat", None, None),
            P(None, "tm", "lat", None, None),
            P(None, "lat", "tm"),
            P("lat", None),
            P("tm"),
            P("tm", "lat", None, None),
            P(),
            P(),
            P("tm", "lat", None, None),
            P("tm", "lat", None, None),
            P("tm", "lat", None, None),
        ),
        out_specs=(P("tm", "lat", None, None), P(None, "lat", "tm")),
        check_vma=False,
    )
```

profile of v0, /device:TPU:0, one launch (start us, length us, event | category | flops | bytes accessed | tf_op | source)
XLA Modules:
  0.0 36.0 jit_solution(5435184335361582618)
XLA Ops:
  1.3 32.2 %shard_map.122 = (f32[1,8,192,128]{3,2,1,0:T(8,128)}, f32[8,128]{1,0:T(8,128)}) custom-call(s32[1]{0:T(128)S(6)} %copy.13.refs_0_, f32[1,8,192,128]{3,2,1,0:T(8,128)} %refs_1_.1, bf16[8,1,8,192,128]{4,3,2,1,0:T(8,128)(2,1)} %refs_2_.1, f32[8,128]{1,0:T(8,128)} %bitcast.1, s32[8,192]{1,0:T(8,128)} %refs_4_.1, bf16[1,8,192,128]{3,2,1,0:T(8,128)(2,1)} %refs_5_.1, ...), custom_call_target="tpu_custom_call" | custom-call | tf_op jit(solution)/shard_map/pallas_call | solution.py:416
  33.4 2.6 %shard_map.123 = (f32[1,8,192,128]{3,2,1,0:T(8,128)}, f32[8,1,128]{2,1,0:T(1,128)}) custom-call(f32[1,8,192,128]{3,2,1,0:T(8,128)} %get-tuple-element.4.grad_h, f32[8,128]{1,0:T(8,128)} %get-tuple-element.5.owned_h), custom_call_target="tpu_custom_call" | custom-call | tf_op jit(solution)/shard_map/pallas_call | solution.py:429
where the time goes:
time: 36.2 us; the launch traced here: 36 us
  Pallas kernels  34.7 us (96%)
  between operations  1.29 us (4%)
    pallas_call x1, Pallas kernels, body(): pl.pallas_call(run, out_shape=(jax.ShapeDtypeStruct(incr.shape, F32), jax...  32.2 us
    pallas_call x1, Pallas kernels, body(): pl.pallas_call(deliver, out_shape=(jax.ShapeDtypeStruct(incr.shape, F32),...  2.57 us

commit v1 on v0

--- a/solution.py
+++ b/solution.py
@@ -23,7 +23,7 @@
     grad_h, gw_ref,
     incr, pert, gathered, cmap, cpad, diff, m_in, m_out, prec, obs, innov,
     onehot, start, start_bf, a_buf, b_buf, state_halo, start_next, prec_next,
-    end_bf, end_prev, u_buf, seed_bf, seed_halo, c_buf, w_buf, mw_t, contrib, grad,
+    end_bf, end_prev, u_buf, seed_bf, seed_halo, c_buf, w_buf, mw_t, contrib,
     term_send, term_recv, local_sem, send_sem, recv_sem, ag_send, ag_recv, rs_send, rs_recv,
 ):
     H, R, LON, LEV, MEM, CW = sizes
@@ -43,7 +43,7 @@
         )
 
     loads = dict(
-        weight=local(0, weight_h, gathered.at[me_t]),
+        weight=local(0, weight_h.at[:, 0], gathered.at[me_t]),
         cmap=local(1, cmap_h, cmap),
         pert=local(2, pert_h.at[:, 0], pert),
         incr=local(3, incr_h.at[0], incr),
@@ -318,12 +318,10 @@
     for i in range(R):
         jump = prec[i].astype(F32) * (start[i] - end_prev[i].astype(F32))
         total = jump + u_buf[i + H]
-        grad[i] = total
+        grad_h[0, i] = total
         terms = jnp.concatenate([(pert[k, i].astype(F32) * total).astype(BF16) for k in range(MEM)], axis=1)
         contrib[:, i * LANES:i * LANES + LON] = lax.dot_general(own, terms, LAST, preferred_element_type=F32)
 
-    store = local(10, grad, grad_h.at[0])
-    store.start()
     sums = lax.dot_general(halves(contrib[...]), onehot[...], LAST, preferred_element_type=F32)
     sums = sums[0:MEM] + sums[MEM:2 * MEM]
     for p in range(tm_count):
@@ -335,7 +333,7 @@
         term(d).wait_recv()
     for d in range(1, tm_count):
         result = result + term_recv[lax.rem(me_t + d, tm_count)]
-    gw_ref[...] = result
+    gw_ref[:, 0, :] = result
 
     for d in range(1, tm_count):
         spread(d).wait_send()
@@ -347,28 +345,16 @@
     sent(prec_back, has_prev)
     sent(start_back, has_prev)
     sent(end_on, has_next)
-    store.wait()
-
-
-def deliver(grad_h, owned_h, out_h, gw_ref, buf, small, sem_in, sem_out, sem_small):
-    R = buf.shape[0]
-    pieces = 4 if R % 4 == 0 else 1
-    size = R // pieces
-    ins, outs = [], []
-    for i in range(pieces):
-        rows = pl.ds(i * size, size)
-        ins.append(pltpu.make_async_copy(grad_h.at[0, rows], buf.at[rows], sem_in.at[i]))
-        outs.append(pltpu.make_async_copy(buf.at[rows], out_h.at[0, rows], sem_out.at[i]))
-    fetch = pltpu.make_async_copy(owned_h, small, sem_small.at[0])
-    for copy in ins:
+
+
+def deliver(grad, owned, grad_h, gw_h, sem):
+    copies = [
+        pltpu.make_async_copy(grad, grad_h, sem.at[0]),
+        pltpu.make_async_copy(owned, gw_h, sem.at[1]),
+    ]
+    for copy in copies:
         copy.start()
-    fetch.start()
-    for arrive, leave in zip(ins, outs):
-        arrive.wait()
-        leave.start()
-    fetch.wait()
-    gw_ref[:, 0, :] = small[...]
-    for copy in outs:
+    for copy in copies:
         copy.wait()
 
 
@@ -402,7 +388,6 @@
             pltpu.VMEM((2, wide, LON, LEV), F32),
             pltpu.VMEM((R * PAD, MEM), F32),
             pltpu.VMEM((MEM, R * PAD), F32),
-            field(R, F32),
             pltpu.VMEM((tm_count, MEM, CW), F32),
             pltpu.VMEM((tm_count, MEM, CW), F32),
             pltpu.SemaphoreType.DMA((11,)),
@@ -413,36 +398,35 @@
         def run(*refs):
             kernel(tm_count, lat_count, (H, R, LON, LEV, MEM, CW), *refs)
 
+        fixed = [
+            pltpu.with_memory_space_constraint(x, pltpu.HBM)
+            for x in (incr, pert, weight, cmap, diffusion, m_in, m_out, prec, obs, innov)
+        ]
         grad, owned = pl.pallas_call(
             run,
             out_shape=(
-                jax.ShapeDtypeStruct(incr.shape, F32),
-                jax.ShapeDtypeStruct((MEM, CW), F32),
+                pltpu.VMEM(incr.shape, F32),
+                pltpu.VMEM((MEM, 1, CW), F32),
             ),
-            in_specs=[pl.BlockSpec(memory_space=pltpu.SMEM)] + [pl.BlockSpec(memory_space=pl.ANY)] * 10,
-            out_specs=(pl.BlockSpec(memory_space=pl.ANY), pl.BlockSpec(memory_space=pltpu.VMEM)),
+            in_specs=[pl.BlockSpec(memory_space=pltpu.SMEM)] + [pl.BlockSpec(memory_space=pltpu.HBM)] * 10,
+            out_specs=(pl.BlockSpec(memory_space=pltpu.VMEM), pl.BlockSpec(memory_space=pltpu.VMEM)),
             scratch_shapes=scratch,
             compiler_params=pltpu.CompilerParams(
-                collective_id=0, has_side_effects=True, vmem_limit_bytes=60 * 1024 * 1024
+                collective_id=0, has_side_effects=True, vmem_limit_bytes=48 * 1024 * 1024
             ),
-        )(steps, incr, pert, weight[:, 0], cmap, diffusion, m_in, m_out, prec, obs, innov)
+        )(steps, *fixed)
+        grad = pltpu.with_memory_space_constraint(grad, pltpu.VMEM)
+        owned = pltpu.with_memory_space_constraint(owned, pltpu.VMEM)
         return pl.pallas_call(
             deliver,
             out_shape=(
                 jax.ShapeDtypeStruct(incr.shape, F32),
                 jax.ShapeDtypeStruct((MEM, 1, CW), F32),
             ),
-            in_specs=[pl.BlockSpec(memory_space=pl.ANY)] * 2,
-            out_specs=(pl.BlockSpec(memory_space=pl.ANY), pl.BlockSpec(memory_space=pltpu.VMEM)),
-            scratch_shapes=[
-                field(R, F32),
-                pltpu.VMEM((MEM, CW), F32),
-                pltpu.SemaphoreType.DMA((4,)),
-                pltpu.SemaphoreType.DMA((4,)),
-                pltpu.SemaphoreType.DMA((1,)),
-            ],
+            in_specs=[pl.BlockSpec(memory_space=pltpu.VMEM)] * 2,
+            out_specs=(pl.BlockSpec(memory_space=pl.ANY), pl.BlockSpec(memory_space=pl.ANY)),
+            scratch_shapes=[pltpu.SemaphoreType.DMA((2,))],
         )(grad, owned)
-
     return jax.shard_map(
         body,
         mesh=mesh,

time: 36.2 us -> 33.9 us (0.936)
  Pallas kernels: 34.7 us -> 32.5 us
    pallas_call x1, Pallas kernels: 2.57 us -> 0.9 us  [body(): pl.pallas_call(deliver, out_shape=(jax.ShapeDtypeStruct(incr.shape, F32),...]
    pallas_call x1, Pallas kernels: 32.2 us -> 31.6 us  [body(): pl.pallas_call(run, out_shape=(pltpu.VMEM(incr.shape, F32), pltpu.VMEM((M...]
where the time goes in v1:
time: 33.9 us; the launch traced here: 33.8 us
  Pallas kernels  32.5 us (96%)
  between operations  1.29 us (4%)
    pallas_call x1, Pallas kernels, body(): pl.pallas_call(run, out_shape=(pltpu.VMEM(incr.shape, F32), pltpu.VMEM((M...  31.6 us
    pallas_call x1, Pallas kernels, body(): pl.pallas_call(deliver, out_shape=(jax.ShapeDtypeStruct(incr.shape, F32),...  0.9 us

profile of v1, /device:TPU:0, one launch (start us, length us, event | category | flops | bytes accessed | tf_op | source)
XLA Modules:
  0.0 33.8 jit_solution(13402928506596110687)
XLA Ops:
  1.3 31.6 %shard_map.122 = (f32[1,8,192,128]{3,2,1,0:T(8,128)S(1)}, f32[8,1,128]{2,1,0:T(1,128)S(1)}) custom-call(s32[1]{0:T(128)S(6)} %copy.13.refs_0_, f32[1,8,192,128]{3,2,1,0:T(8,128)} %refs_1_.1, bf16[8,1,8,192,128]{4,3,2,1,0:T(8,128)(2,1)} %refs_2_.1, f32[8,1,128]{2,1,0:T(1,128)} %refs_3_.1, s32[8,192]{1,0:T(8,128)} %refs_4_.1, ...), custom_call_target="tpu_custom_call" | custom-call | tf_op jit(solution)/shard_map/pallas_call | solution.py:405
  32.9 0.9 %shard_map.123 = (f32[1,8,192,128]{3,2,1,0:T(8,128)}, f32[8,1,128]{2,1,0:T(1,128)}) custom-call(f32[1,8,192,128]{3,2,1,0:T(8,128)S(1)} %get-tuple-element.4.grad, f32[8,1,128]{2,1,0:T(1,128)S(1)} %get-tuple-element.5.owned), custom_call_target="tpu_custom_call" | custom-call | tf_op jit(solution)/shard_map/pallas_call | solution.py:420

commit v2 on v1

v2 whole, which is shorter than its diff:
```python
import jax
import jax.numpy as jnp
from jax import lax
from jax.experimental import pallas as pl
from jax.experimental.pallas import tpu as pltpu
from jax.sharding import PartitionSpec as P

MESH = pl.DeviceIdType.MESH
F32, BF16 = jnp.float32, jnp.bfloat16
EDGE = 8
LANES = 128
WIDTH = 256


def supplied(k):
    return k // 2, k // 2 + k % 2 + 1


def kernel(
    tm_count, lat_count, sizes,
    steps_ref, incr_h, pert_h, weight_h, cmap_h, diff_h, min_h, mout_h, prec_h, obs_h, innov_h,
    grad_ref, gw_ref,
    incr, pert, gathered, cmap, diff, diff_halo, d_buf, e_buf, m_in, m_out, prec, obs, innov,
    both, both_t, cflat, sums_buf, onehot, start, start_bf, s_buf, w_buf, u_buf, ec_buf, end_buf, end_bf, end_prev, start_next, prec_next,
    fwd_send, fwd_recv, adj_send, adj_recv, contrib,
    term_send, term_recv, local_sem, send_sem, recv_sem, ag_send, ag_recv, rs_send, rs_recv,
):
    H, R, LON, LEV, MEM, CW = sizes
    C = CW * tm_count
    D = diff_halo.shape[1]
    DS = (s_buf.shape[1] - R) // 2
    HALF = R // 2
    GJ = WIDTH // MEM
    me_t, me_l = lax.axis_index("tm"), lax.axis_index("lat")
    has_up, has_down = me_l > 0, me_l < lat_count - 1
    has_prev, has_next = me_t > 0, me_t < tm_count - 1

    def pair(r):
        return (r, R - 1 - r)

    def local(i, src, dst):
        return pltpu.make_async_copy(src, dst, local_sem.at[i])

    count = [0]

    def remote(src, dst, tm, lat):
        i = count[0]
        count[0] += 1
        return pltpu.make_async_remote_copy(
            src_ref=src, dst_ref=dst, send_sem=send_sem.at[i], recv_sem=recv_sem.at[i],
            device_id=(tm, lat), device_id_type=MESH,
        )

    loads = dict(
        weight=local(0, weight_h.at[:, 0], gathered.at[me_t]),
        cmap=local(1, cmap_h, cmap),
        diff=local(2, diff_h.at[0], diff),
        pert=local(3, pert_h.at[:, 0], pert),
        incr=local(4, incr_h.at[0], incr),
        m_in=local(5, min_h, m_in),
        m_out=local(6, mout_h, m_out),
        obs=local(7, obs_h.at[0], obs),
        innov=local(8, innov_h.at[0], innov),
        prec=local(9, prec_h.at[0], prec),
    )
    barrier = pltpu.get_barrier_semaphore()
    for d in range(1, tm_count):
        pl.semaphore_signal(barrier, inc=1, device_id=(lax.rem(me_t + d, tm_count), me_l), device_id_type=MESH)

    @pl.when(has_up)
    def _():
        pl.semaphore_signal(barrier, inc=1, device_id=(me_t, me_l - 1), device_id_type=MESH)

    @pl.when(has_down)
    def _():
        pl.semaphore_signal(barrier, inc=1, device_id=(me_t, me_l + 1), device_id_type=MESH)

    for copy in loads.values():
        copy.start()

    def clear(side):
        diff_halo[side] = jnp.zeros((D, LON, LEV), BF16)
        fwd_recv[side] = jnp.zeros((H, LON, LEV), BF16)
        adj_recv[side] = jnp.zeros((H, LON, LEV), BF16)

    @pl.when(jnp.logical_not(has_up))
    def _():
        clear(0)

    @pl.when(jnp.logical_not(has_down))
    def _():
        clear(1)

    @pl.when(jnp.logical_not(has_prev))
    def _():
        end_prev[...] = jnp.zeros((R, LON, LEV), BF16)

    @pl.when(jnp.logical_not(has_next))
    def _():
        start_next[...] = jnp.zeros((R, LON, LEV), BF16)
        prec_next[...] = jnp.zeros((R, LON, LEV), BF16)

    loads["weight"].wait()
    pl.semaphore_wait(barrier, tm_count - 1 + has_up.astype(jnp.int32) + has_down.astype(jnp.int32))

    def spread(d):
        peer = lax.rem(me_t + d, tm_count)
        return pltpu.make_async_remote_copy(
            src_ref=gathered.at[me_t], dst_ref=gathered.at[me_t], send_sem=ag_send.at[d],
            recv_sem=ag_recv.at[d], device_id=(peer, me_l), device_id_type=MESH,
        )

    def term(d):
        peer = lax.rem(me_t + d, tm_count)
        return pltpu.make_async_remote_copy(
            src_ref=term_send.at[peer], dst_ref=term_recv.at[me_t], send_sem=rs_send.at[d],
            recv_sem=rs_recv.at[d], device_id=(peer, me_l), device_id_type=MESH,
        )

    for d in range(1, tm_count):
        spread(d).start()

    diff_up = remote(diff_h.at[0, pl.ds(0, D)], diff_halo.at[1], me_t, me_l - 1)
    diff_down = remote(diff_h.at[0, pl.ds(R - D, D)], diff_halo.at[0], me_t, me_l + 1)
    prec_back = [remote(prec_h.at[0, i], prec_next.at[i], me_t - 1, me_l) for i in range(R)]
    start_back = [remote(start_bf.at[i], start_next.at[i], me_t - 1, me_l) for i in range(R)]
    end_on = [remote(end_bf.at[i], end_prev.at[i], me_t + 1, me_l) for i in range(R)]
    fwd_up, fwd_down, adj_up, adj_down = [], [], [], []
    for k in range(H):
        n, depth = supplied(k)
        first, last = depth - 1, R - depth
        up_src = start_bf.at[first] if n == 0 else fwd_send.at[0, k]
        down_src = start_bf.at[last] if n == 0 else fwd_send.at[1, k]
        fwd_up.append(remote(up_src, fwd_recv.at[1, k], me_t, me_l - 1))
        fwd_down.append(remote(down_src, fwd_recv.at[0, k], me_t, me_l + 1))
        adj_up.append(remote(adj_send.at[0, k], adj_recv.at[1, k], me_t, me_l - 1))
        adj_down.append(remote(adj_send.at[1, k], adj_recv.at[0, k], me_t, me_l + 1))

    def go(there, *copies):
        @pl.when(there)
        def _():
            for copy in copies:
                copy.start()

    def sent(there, *copies):
        @pl.when(there)
        def _():
            for copy in copies:
                copy.wait_send()

    def got(there, *copies):
        @pl.when(there)
        def _():
            for copy in copies:
                copy.wait_recv()

    def rows_of(copies, r):
        return [copies[i] for i in pair(r)]

    go(has_up, diff_up)
    go(has_down, diff_down)
    early = [r for r in (1, 0, 2) if r < HALF]
    late = [r for r in range(HALF) if r not in early]
    for r in early:
        go(has_prev, *rows_of(prec_back, r))

    loads["cmap"].wait()
    for r in range(HALF):
        for s, i in enumerate(pair(r)):
            at = (2 * r + s) * LON
            cflat[:, at:at + LON] = cmap[i:i + 1, :]
    for c in range(0, C, LANES):
        rows = lax.broadcasted_iota(jnp.int32, (LANES, R * LON), 0) + c
        onehot[c:c + LANES, :] = jnp.where(rows == cflat[...], 1.0, 0.0).astype(BF16)
    loads["diff"].wait()

    def widen_diff(value, i):
        wide = value.astype(F32)
        d_buf[i] = wide
        e_buf[i] = 1.0 - 4.0 * wide

    for i in range(R):
        widen_diff(diff[i], i + D)
    loads["pert"].wait()
    loads["incr"].wait()
    loads["m_in"].wait()
    loads["m_out"].wait()
    for n in range(H):
        product = jnp.dot(m_in[n], m_out[n], preferred_element_type=F32)
        both[n] = product.astype(BF16)
        both_t[n] = jnp.transpose(product).astype(BF16)
    loads["obs"].wait()
    loads["innov"].wait()
    loads["prec"].wait()
    step_count = steps_ref[0]

    def put(buf, n, i, value):
        buf[n, i, EDGE:EDGE + LON] = value
        buf[n, i, EDGE - 1:EDGE] = value[LON - 1:LON]
        buf[n, i, EDGE + LON:EDGE + LON + 1] = value[0:1]

    def around(buf, n, i):
        north, south = buf[n, i - 1, EDGE:EDGE + LON], buf[n, i + 1, EDGE:EDGE + LON]
        west, east = buf[n, i, EDGE - 1:EDGE - 1 + LON], buf[n, i, EDGE + 1:EDGE + 1 + LON]
        return (north + south) + (west + east)

    def fwd_row(n, r, value, send=True):
        for s, i in enumerate(pair(r)):
            put(s_buf, n, i + DS, value[s])
        for k in range(H):
            if send and supplied(k) == (n, r + 1):
                if n > 0:
                    for s in range(2):
                        fwd_send[s, k] = value[s].astype(BF16)
                go(has_up, fwd_up[k])
                go(has_down, fwd_down[k])

    row = lax.broadcasted_iota(jnp.int32, (GJ, WIDTH), 0)
    lane = lax.broadcasted_iota(jnp.int32, (GJ, WIDTH), 1)
    own_cell = lax.rem(lane, GJ) == row
    groups = LON // GJ

    def places(r):
        found = []
        for at in range(2 * r * LON, 2 * (r + 1) * LON, LANES):
            index = jnp.broadcast_to(cflat[:, at:at + LANES], (MEM, LANES))
            found.append((index // LANES, index % LANES))
        return found

    placed = [places(r) for r in range(HALF)]
    repeat_row = lax.broadcasted_iota(jnp.int32, (MEM, WIDTH), 0)
    repeat_lane = lax.broadcasted_iota(jnp.int32, (MEM, WIDTH), 1) // GJ
    repeat = jnp.where(repeat_row == repeat_lane, 1.0, 0.0).astype(BF16)

    for d in range(1, tm_count):
        spread(d).wait_recv()
    weights = jnp.concatenate([gathered[p] for p in range(tm_count)], axis=1)
    def pick(r):
        found = []
        for block, inside in placed[r]:
            value = jnp.zeros((MEM, LANES), F32)
            for c in range(C // LANES):
                taken = jnp.take_along_axis(weights[:, c * LANES:(c + 1) * LANES], inside, axis=1)
                value = jnp.where(block == c, taken, value)
            found.append(jnp.transpose(value))
        return jnp.concatenate(found, axis=0).astype(BF16)

    def begin(r):
        cells = pick(r)
        picked = jnp.dot(cells, repeat, preferred_element_type=F32)
        value = []
        for s, i in enumerate(pair(r)):
            pieces = []
            for g in range(groups):
                at = g * GJ
                block = jnp.where(own_cell, picked[s * LON + at:s * LON + at + GJ], 0.0).astype(BF16)
                members = pert[:, i, at:at + GJ, :].reshape(WIDTH, LEV)
                pieces.append(incr[i, at:at + GJ] + jnp.dot(block, members, preferred_element_type=F32))
            state = jnp.concatenate(pieces, axis=0)
            start[i] = state
            start_bf[i] = state.astype(BF16)
            value.append(state)
        fwd_row(0, r, value)
        go(has_prev, *rows_of(start_back, r))

    def modes(value, both):
        flat = jnp.concatenate([v.astype(BF16) for v in value], axis=0)
        moved = jnp.dot(flat, both, preferred_element_type=F32)
        return [value[s] + moved[s * LON:(s + 1) * LON] for s in range(2)]

    def step(n, r):
        here = [s_buf[n, i + DS, EDGE:EDGE + LON] for i in pair(r)]
        smoothed = [e_buf[i + D] * here[s] + d_buf[i + D] * around(s_buf, n, i + DS) for s, i in enumerate(pair(r))]
        result = modes(smoothed, both[n])
        if n > 0:
            result = [jnp.where(n < step_count, a, b) for a, b in zip(result, here)]
        if n + 1 < H:
            fwd_row(n + 1, r, result)
        else:
            for s, i in enumerate(pair(r)):
                end_buf[i] = result[s]
                end_bf[i] = result[s].astype(BF16)
            go(has_next, *rows_of(end_on, r))

    def fold(r):
        return R - 1 - r if r >= HALF else r

    def needs_state(n, r, found):
        if (n, r) in found:
            return
        found.add((n, r))
        if n == 0 or (r < 0 and n <= -r - 1):
            return
        for near in (r - 1, r, r + 1):
            needs_state(n - 1, fold(near), found)

    wanted = set()
    for r in range(HALF):
        needs_state(H, r, wanted)
    known = set()

    def forward():
        while True:
            ready = [
                (n, r) for n, r in sorted(wanted) if (n, r) not in known and n > 0
                and not (r < 0 and n <= -r - 1)
                and all((n - 1, fold(q)) in known for q in (r - 1, r, r + 1))
            ]
            if not ready:
                return
            for n, r in ready:
                step(n - 1, r)
                known.add((n, r))

    for r in range(HALF):
        begin(r)
        known.add((0, r))
        if r == max(early):
            for q in late:
                go(has_prev, *rows_of(prec_back, q))
        forward()

    wanted_u, wanted_w = set(), set()

    def needs_u(m, r):
        if (m, r) in wanted_u:
            return
        wanted_u.add((m, r))
        if m == 0 or (r < 0 and m <= -r - 1):
            return
        needs_u(m - 1, r)
        for near in (r - 1, r, r + 1):
            needs_w(m - 1, fold(near))

    def needs_w(m, r):
        if (m, r) in wanted_w:
            return
        wanted_w.add((m, r))
        if not (r < 0 and m <= -r - 1):
            needs_u(m, r)

    for r in range(HALF):
        needs_u(H, r)
    known_u, known_w, coupled_at = set(), set(), set()

    def adj_send_row(k, value):
        for s in range(2):
            adj_send[s, k] = value[s].astype(BF16)
        go(has_up, adj_up[k])
        go(has_down, adj_down[k])

    def have_u(m, r, value):
        for s, i in enumerate(pair(r)):
            u_buf[i + D] = value[s]
        known_u.add((m, r))
        for k in range(0, H, 2):
            if r >= 0 and supplied(k) == (m, r + 1):
                adj_send_row(k, value)

    def couple(m, r):
        n = H - 1 - m
        here = [u_buf[i + D] for i in pair(r)]
        coupled = modes(here, both_t[n])
        weighted = [d_buf[i + D] * coupled[s] for s, i in enumerate(pair(r))]
        for s, i in enumerate(pair(r)):
            ec_buf[i + D] = e_buf[i + D] * coupled[s]
            put(w_buf, m, i + DS, weighted[s])
        for k in range(1, H, 2):
            if r >= 0 and supplied(k) == (m, r + 1):
                adj_send_row(k, weighted)

    def settle(m, r):
        value = []
        for s, i in enumerate(pair(r)):
            result = ec_buf[i + D] + around(w_buf, m, i + DS)
            if m < H - 1:
                result = jnp.where(H - 1 - m < step_count, result, u_buf[i + D])
            value.append(result)
        if m + 1 < H:
            have_u(m + 1, r, value)
        else:
            known_u.add((H, r))
            final(r, value)

    level_row = lax.broadcasted_iota(jnp.int32, (MEM * LEV, 2 * MEM), 0) // LEV
    level_lane = lax.broadcasted_iota(jnp.int32, (MEM * LEV, 2 * MEM), 1) % MEM
    own = jnp.where(level_row == level_lane, 1.0, 0.0).astype(BF16)
    is_high = lax.broadcasted_iota(jnp.int32, (2 * LON, 2 * MEM), 1) < MEM
    cut = max(HALF // 2, 1)
    parts = [list(range(0, cut)), list(range(cut, HALF))]
    totals = []

    def final(r, value):
        got(has_prev, *rows_of(end_on, r))
        terms = []
        for s, i in enumerate(pair(r)):
            total = prec[i].astype(F32) * (start[i] - end_prev[i].astype(F32)) + value[s]
            grad_ref[0, i] = total
            rounded = total.astype(BF16)
            terms.append(jnp.concatenate([pert[k, i] * rounded for k in range(MEM)], axis=1))
        summed = jnp.concatenate([jnp.dot(t, own, preferred_element_type=F32) for t in terms], axis=0)
        high = summed.astype(BF16).astype(F32)
        at = 2 * r * LON
        contrib[at:at + 2 * LON] = jnp.where(is_high, high, summed - high).astype(BF16)
        for part in parts:
            if r in part and all((H, q) in known_u for q in part):
                at, until = 2 * part[0] * LON, 2 * (part[-1] + 1) * LON
                share = jnp.dot(onehot[:, at:until], contrib[at:until], preferred_element_type=F32)
                if totals:
                    share = share + sums_buf[...]
                sums_buf[...] = share
                totals.append(part)

    def leading(goals):
        need_c, need_s, stack = set(), set(), []
        for m, r in goals:
            stack.append(("c" if (m, r + 1) in [supplied(k) for k in range(1, H, 2)] else "u", m, r))
        while stack:
            kind, m, r = stack.pop()
            if kind == "c" and (m, r) not in need_c:
                need_c.add((m, r))
                stack.append(("u", m, r))
            elif kind == "u" and m > 0 and (m - 1, r) not in need_s:
                need_s.add((m - 1, r))
                stack.extend(("c", m - 1, fold(q)) for q in (r - 1, r, r + 1))
        return need_c, need_s

    def adjoint(goals=None):
        only = leading(goals) if goals else None
        while True:
            ready = [("c", m, r) for m, r in sorted(known_u) if m < H and (m, r) not in coupled_at
                     and ((m, r) in wanted_w or (m + 1, r) in wanted_u)]
            ready += [
                ("s", m - 1, r) for m, r in sorted(wanted_u) if m > 0 and (m, r) not in known_u
                and not (r < 0 and m <= -r - 1) and (m - 1, r) in coupled_at
                and all((m - 1, fold(q)) in known_w for q in (r - 1, r, r + 1))
            ]
            if only:
                ready = [t for t in ready if t[1:] in only[0 if t[0] == "c" else 1]]
            if not ready:
                return
            for kind, m, r in ready:
                if kind == "c":
                    couple(m, r)
                    coupled_at.add((m, r))
                    known_w.add((m, r))
                else:
                    settle(m, r)

    def seed(r):
        value = []
        for i in pair(r):
            end = end_buf[i]
            misfit = obs[i].astype(F32) * (end - innov[i].astype(F32))
            value.append(misfit - prec_next[i].astype(F32) * (start_next[i].astype(F32) - end))
        have_u(0, r, value)

    got(has_down, diff_up)
    got(has_up, diff_down)
    for q in range(1, D + 1):
        widen_diff(diff_halo[0, D - q], D - q)
        widen_diff(diff_halo[1, q - 1], R - 1 + D + q)

    urgent = {(supplied(k)[0], supplied(k)[1] - 1) for k in range(H)}

    def seed_and_send(r):
        got(has_next, *rows_of(prec_back, r), *rows_of(start_back, r))
        seed(r)
        adjoint(urgent)

    split = max(H - 2, 0)
    seeded = []
    for some in [range(split)] + [range(k, k + 1) for k in range(split, H)]:
        for k in some:
            got(has_down, fwd_up[k])
            got(has_up, fwd_down[k])
        for k in some:
            n, depth = supplied(k)
            fwd_row(n, -depth, [fwd_recv[s, k].astype(F32) for s in range(2)], send=False)
            known.add((n, -depth))
        forward()
        if (H, 1) in known and not seeded:
            seed_and_send(1)
            seeded.append(1)
    for r in range(HALF):
        if r not in seeded:
            seed_and_send(r)
    adjoint()

    order = [1, 0] + list(range(2, H)) if H > 1 else [0]
    for first in range(0, H, 2):
        some = order[first:first + 2]
        for k in some:
            got(has_down, adj_up[k])
            got(has_up, adj_down[k])
        for k in some:
            m, depth = supplied(k)
            value = [adj_recv[s, k].astype(F32) for s in range(2)]
            if k % 2 == 0:
                have_u(m, -depth, value)
            else:
                for s, i in enumerate(pair(-depth)):
                    put(w_buf, m, i + DS, value[s])
                known_w.add((m, -depth))
        adjoint()

    sums = jnp.transpose(sums_buf[...])
    sums = sums[0:MEM] + sums[MEM:2 * MEM]
    for p in range(tm_count):
        term_send[p] = sums[:, p * CW:(p + 1) * CW]
    for d in range(1, tm_count):
        term(d).start()
    result = gathered[me_t] + term_send[me_t]
    for d in range(1, tm_count):
        term(d).wait_recv()
    for d in range(1, tm_count):
        result = result + term_recv[lax.rem(me_t + d, tm_count)]
    gw_ref[:, 0, :] = result

    for d in range(1, tm_count):
        spread(d).wait_send()
        term(d).wait_send()
    sent(has_up, diff_up, *fwd_up, *adj_up)
    sent(has_down, diff_down, *fwd_down, *adj_down)
    sent(has_prev, *prec_back, *start_back)
    sent(has_next, *end_on)


def deliver(grad, owned, grad_h, gw_h, sem):
    copies = [
        pltpu.make_async_copy(grad, grad_h, sem.at[0]),
        pltpu.make_async_copy(owned, gw_h, sem.at[1]),
    ]
    for copy in copies:
        copy.start()
    for copy in copies:
        copy.wait()


def solution(mesh):
    tm_count, lat_count = mesh.shape["tm"], mesh.shape["lat"]

    def body(incr, pert, weight, cmap, steps, diffusion, m_in, m_out, prec, obs, innov):
        _, R, LON, LEV = incr.shape
        MEM, _, CW = weight.shape
        H = m_in.shape[0]
        D = max(H // 2, 1)
        DS = max(supplied(k)[1] for k in range(H))
        C = CW * tm_count
        field = lambda rows, kind: pltpu.VMEM((rows, LON, LEV), kind)
        padded = pltpu.VMEM((H, R + 2 * DS, LON + 2 * EDGE, LEV), F32)
        halo = pltpu.VMEM((2, H, LON, LEV), BF16)
        scratch = [
            field(R, F32),
            pltpu.VMEM((MEM, R, LON, LEV), BF16),
            pltpu.VMEM((tm_count, MEM, CW), F32),
            pltpu.VMEM((R, LON), jnp.int32),
            field(R, BF16),
            pltpu.VMEM((2, D, LON, LEV), BF16),
            field(R + 2 * D, F32), field(R + 2 * D, F32),
            pltpu.VMEM(m_in.shape, BF16),
            pltpu.VMEM(m_out.shape, BF16),
            field(R, BF16), field(R, BF16), field(R, BF16),
            pltpu.VMEM((H, LEV, LEV), BF16),
            pltpu.VMEM((H, LEV, LEV), BF16),
            pltpu.VMEM((1, R * LON), jnp.int32),
            pltpu.VMEM((C, 2 * MEM), F32),
            pltpu.VMEM((C, R * LON), BF16),
            field(R, F32), field(R, BF16), padded, padded,
            field(R + 2 * D, F32), field(R + 2 * D, F32),
            field(R, F32), field(R, BF16), field(R, BF16), field(R, BF16), field(R, BF16),
            halo, halo, halo, halo,
            pltpu.VMEM((R * LON, 2 * MEM), BF16),
            pltpu.VMEM((tm_count, MEM, CW), F32),
            pltpu.VMEM((tm_count, MEM, CW), F32),
            pltpu.SemaphoreType.DMA((10,)),
            pltpu.SemaphoreType.DMA((2 + 3 * R + 4 * H,)),
            pltpu.SemaphoreType.DMA((2 + 3 * R + 4 * H,)),
        ] + [pltpu.SemaphoreType.DMA((tm_count,))] * 4

        def run(*refs):
            kernel(tm_count, lat_count, (H, R, LON, LEV, MEM, CW), *refs)

        fixed = [
            pltpu.with_memory_space_constraint(x, pltpu.HBM)
            for x in (incr, pert, weight, cmap, diffusion, m_in, m_out, prec, obs, innov)
        ]
        grad, owned = pl.pallas_call(
            run,
            out_shape=(
                pltpu.VMEM(incr.shape, F32),
                pltpu.VMEM((MEM, 1, CW), F32),
            ),
            in_specs=[pl.BlockSpec(memory_space=pltpu.SMEM)] + [pl.BlockSpec(memory_space=pltpu.HBM)] * 10,
            out_specs=(pl.BlockSpec(memory_space=pltpu.VMEM), pl.BlockSpec(memory_space=pltpu.VMEM)),
            scratch_shapes=scratch,
            compiler_params=pltpu.CompilerParams(
                collective_id=0, has_side_effects=True, vmem_limit_bytes=48 * 1024 * 1024
            ),
        )(steps, *fixed)
        grad = pltpu.with_memory_space_constraint(grad, pltpu.VMEM)
        owned = pltpu.with_memory_space_constraint(owned, pltpu.VMEM)
        return pl.pallas_call(
            deliver,
            out_shape=(
                jax.ShapeDtypeStruct(incr.shape, F32),
                jax.ShapeDtypeStruct((MEM, 1, CW), F32),
            ),
            in_specs=[pl.BlockSpec(memory_space=pltpu.VMEM)] * 2,
            out_specs=(pl.BlockSpec(memory_space=pl.ANY), pl.BlockSpec(memory_space=pl.ANY)),
            scratch_shapes=[pltpu.SemaphoreType.DMA((2,))],
        )(grad, owned)

    return jax.shard_map(
        body,
        mesh=mesh,
        in_specs=(
            P("tm", "lat", None, None),
            P(None, "tm", "lat", None, None),
            P(None, "lat", "tm"),
            P("lat", None),
            P("tm"),
            P("tm", "lat", None, None),
            P(),
            P(),
            P("tm", "lat", None, None),
            P("tm", "lat", None, None),
            P("tm", "lat", None, None),
        ),
        out_specs=(P("tm", "lat", None, None), P(None, "lat", "tm")),
        check_vma=False,
    )
```

time: 33.9 us -> 30.9 us (0.912)
  Pallas kernels: 32.5 us -> 29.5 us
    pallas_call x1, Pallas kernels: 31.6 us -> 28.6 us  [body(): pl.pallas_call(run, out_shape=(pltpu.VMEM(incr.shape, F32), pltpu.VMEM((M...]
where the time goes in v2:
time: 30.9 us; the launch traced here: 30.7 us
  Pallas kernels  29.5 us (95%)
  between operations  1.29 us (4%)
    pallas_call x1, Pallas kernels, body(): pl.pallas_call(run, out_shape=(pltpu.VMEM(incr.shape, F32), pltpu.VMEM((M...  28.6 us
    pallas_call x1, Pallas kernels, body(): pl.pallas_call(deliver, out_shape=(jax.ShapeDtypeStruct(incr.shape, F32),...  0.9 us

profile of v2, /device:TPU:0, one launch (start us, length us, event | category | flops | bytes accessed | tf_op | source)
XLA Modules:
  0.0 30.7 jit_solution(18433197857483641335)
XLA Ops:
  1.3 28.6 %shard_map.122 = (f32[1,8,192,128]{3,2,1,0:T(8,128)S(1)}, f32[8,1,128]{2,1,0:T(1,128)S(1)}) custom-call(s32[1]{0:T(128)S(6)} %copy.13.refs_0_, f32[1,8,192,128]{3,2,1,0:T(8,128)} %refs_1_.1, bf16[8,1,8,192,128]{4,3,2,1,0:T(8,128)(2,1)} %refs_2_.1, f32[8,1,128]{2,1,0:T(1,128)} %refs_3_.1, s32[8,192]{1,0:T(8,128)} %refs_4_.1, ...), custom_call_target="tpu_custom_call" | custom-call | tf_op jit(solution)/shard_map/pallas_call | solution.py:588
  29.8 0.9 %shard_map.123 = (f32[1,8,192,128]{3,2,1,0:T(8,128)}, f32[8,1,128]{2,1,0:T(1,128)}) custom-call(f32[1,8,192,128]{3,2,1,0:T(8,128)S(1)} %get-tuple-element.4.grad, f32[8,1,128]{2,1,0:T(1,128)S(1)} %get-tuple-element.5.owned), custom_call_target="tpu_custom_call" | custom-call | tf_op jit(solution)/shard_map/pallas_call | solution.py:603

commit v3 on v2

--- a/solution.py
+++ b/solution.py
@@ -21,9 +21,9 @@
     steps_ref, incr_h, pert_h, weight_h, cmap_h, diff_h, min_h, mout_h, prec_h, obs_h, innov_h,
     grad_ref, gw_ref,
     incr, pert, gathered, cmap, diff, diff_halo, d_buf, e_buf, m_in, m_out, prec, obs, innov,
-    both, both_t, cflat, sums_buf, onehot, start, start_bf, s_buf, w_buf, u_buf, ec_buf, end_buf, end_bf, end_prev, start_next, prec_next,
-    fwd_send, fwd_recv, adj_send, adj_recv, contrib,
-    term_send, term_recv, local_sem, send_sem, recv_sem, ag_send, ag_recv, rs_send, rs_recv,
+    both, both_t, cflat, sums_buf, in_group, in_lane, start, start_bf, s_buf, w_buf, u_buf, ec_buf, end_buf, end_bf, end_prev, start_next, prec_next,
+    fwd_send, fwd_recv, adj_send, adj_recv,
+    term_send, term_recv, local_sem, send_sem, recv_sem,
 ):
     H, R, LON, LEV, MEM, CW = sizes
     C = CW * tm_count
@@ -31,6 +31,7 @@
     DS = (s_buf.shape[1] - R) // 2
     HALF = R // 2
     GJ = WIDTH // MEM
+    GL, HB = min(GJ, CW), CW // min(GJ, CW)
     me_t, me_l = lax.axis_index("tm"), lax.axis_index("lat")
     has_up, has_down = me_l > 0, me_l < lat_count - 1
     has_prev, has_next = me_t > 0, me_t < tm_count - 1
@@ -41,15 +42,17 @@
     def local(i, src, dst):
         return pltpu.make_async_copy(src, dst, local_sem.at[i])
 
-    count = [0]
-
-    def remote(src, dst, tm, lat):
-        i = count[0]
-        count[0] += 1
+    def remote(src, dst, tm, lat, out, into):
         return pltpu.make_async_remote_copy(
-            src_ref=src, dst_ref=dst, send_sem=send_sem.at[i], recv_sem=recv_sem.at[i],
+            src_ref=src, dst_ref=dst, send_sem=send_sem.at[out], recv_sem=recv_sem.at[into],
             device_id=(tm, lat), device_id_type=MESH,
         )
+
+    def all_sent(out, ref):
+        remote(ref, ref, me_t, me_l, out, 0).wait_send()
+
+    def all_here(into, ref):
+        remote(ref, ref, me_t, me_l, 0, into).wait_recv()
 
     loads = dict(
         weight=local(0, weight_h.at[:, 0], gathered.at[me_t]),
@@ -103,38 +106,51 @@
     loads["weight"].wait()
     pl.semaphore_wait(barrier, tm_count - 1 + has_up.astype(jnp.int32) + has_down.astype(jnp.int32))
 
+    others = pl.ds(0, tm_count - 1)
+
     def spread(d):
         peer = lax.rem(me_t + d, tm_count)
-        return pltpu.make_async_remote_copy(
-            src_ref=gathered.at[me_t], dst_ref=gathered.at[me_t], send_sem=ag_send.at[d],
-            recv_sem=ag_recv.at[d], device_id=(peer, me_l), device_id_type=MESH,
-        )
+        return remote(gathered.at[me_t], gathered.at[me_t], peer, me_l, 0, 0)
 
     def term(d):
         peer = lax.rem(me_t + d, tm_count)
-        return pltpu.make_async_remote_copy(
-            src_ref=term_send.at[peer], dst_ref=term_recv.at[me_t], send_sem=rs_send.at[d],
-            recv_sem=rs_recv.at[d], device_id=(peer, me_l), device_id_type=MESH,
-        )
+        return remote(term_send.at[peer], term_recv.at[me_t], peer, me_l, 1, 1)
 
     for d in range(1, tm_count):
         spread(d).start()
 
-    diff_up = remote(diff_h.at[0, pl.ds(0, D)], diff_halo.at[1], me_t, me_l - 1)
-    diff_down = remote(diff_h.at[0, pl.ds(R - D, D)], diff_halo.at[0], me_t, me_l + 1)
-    prec_back = [remote(prec_h.at[0, i], prec_next.at[i], me_t - 1, me_l) for i in range(R)]
-    start_back = [remote(start_bf.at[i], start_next.at[i], me_t - 1, me_l) for i in range(R)]
-    end_on = [remote(end_bf.at[i], end_prev.at[i], me_t + 1, me_l) for i in range(R)]
+    early_groups = [list(range(max(H - 2, 0)))] + [[k] for k in range(max(H - 2, 0), H)]
+    adj_order = [1, 0] + list(range(2, H)) if H > 1 else [0]
+    late_groups = [adj_order[k:k + 2] for k in range(0, H, 2)]
+    early_groups = [g for g in early_groups if g]
+    fwd_sem = {k: 4 + 2 * g for g, group in enumerate(early_groups) for k in group}
+    adj_base = 4 + 2 * len(early_groups)
+    adj_sem = {k: adj_base + 2 * g for g, group in enumerate(late_groups) for k in group}
+    next_base = adj_base + 2 * len(late_groups)
+    prev_base = next_base + HALF
+
+    def pair_of(i):
+        return min(i, R - 1 - i)
+
+    diff_up = remote(diff_h.at[0, pl.ds(0, D)], diff_halo.at[1], me_t, me_l - 1, 2, 2)
+    diff_down = remote(diff_h.at[0, pl.ds(R - D, D)], diff_halo.at[0], me_t, me_l + 1, 3, 3)
+    prec_back = [
+        remote(prec_h.at[0, i], prec_next.at[i], me_t - 1, me_l, 4, next_base + pair_of(i)) for i in range(R)
+    ]
+    start_back = [
+        remote(start_bf.at[i], start_next.at[i], me_t - 1, me_l, 5, next_base + pair_of(i)) for i in range(R)
+    ]
+    end_on = [remote(end_bf.at[i], end_prev.at[i], me_t + 1, me_l, 6, prev_base + pair_of(i)) for i in range(R)]
     fwd_up, fwd_down, adj_up, adj_down = [], [], [], []
     for k in range(H):
         n, depth = supplied(k)
         first, last = depth - 1, R - depth
         up_src = start_bf.at[first] if n == 0 else fwd_send.at[0, k]
         down_src = start_bf.at[last] if n == 0 else fwd_send.at[1, k]
-        fwd_up.append(remote(up_src, fwd_recv.at[1, k], me_t, me_l - 1))
-        fwd_down.append(remote(down_src, fwd_recv.at[0, k], me_t, me_l + 1))
-        adj_up.append(remote(adj_send.at[0, k], adj_recv.at[1, k], me_t, me_l - 1))
-        adj_down.append(remote(adj_send.at[1, k], adj_recv.at[0, k], me_t, me_l + 1))
+        fwd_up.append(remote(up_src, fwd_recv.at[1, k], me_t, me_l - 1, 7, fwd_sem[k]))
+        fwd_down.append(remote(down_src, fwd_recv.at[0, k], me_t, me_l + 1, 8, fwd_sem[k] + 1))
+        adj_up.append(remote(adj_send.at[0, k], adj_recv.at[1, k], me_t, me_l - 1, 9, adj_sem[k]))
+        adj_down.append(remote(adj_send.at[1, k], adj_recv.at[0, k], me_t, me_l + 1, 10, adj_sem[k] + 1))
 
     def go(there, *copies):
         @pl.when(there)
@@ -142,17 +158,17 @@
             for copy in copies:
                 copy.start()
 
-    def sent(there, *copies):
+    def sent(there, *waits):
         @pl.when(there)
         def _():
-            for copy in copies:
-                copy.wait_send()
-
-    def got(there, *copies):
+            for out, ref in waits:
+                all_sent(out, ref)
+
+    def got(there, *waits):
         @pl.when(there)
         def _():
-            for copy in copies:
-                copy.wait_recv()
+            for into, ref in waits:
+                all_here(into, ref)
 
     def rows_of(copies, r):
         return [copies[i] for i in pair(r)]
@@ -169,9 +185,14 @@
         for s, i in enumerate(pair(r)):
             at = (2 * r + s) * LON
             cflat[:, at:at + LON] = cmap[i:i + 1, :]
-    for c in range(0, C, LANES):
-        rows = lax.broadcasted_iota(jnp.int32, (LANES, R * LON), 0) + c
-        onehot[c:c + LANES, :] = jnp.where(rows == cflat[...], 1.0, 0.0).astype(BF16)
+    high_row = lax.broadcasted_iota(jnp.int32, (C // GL, R * LON), 0)
+    in_group[...] = jnp.where(high_row == cflat[...] // GL, 1.0, 0.0).astype(BF16)
+    low_lane = lax.rem(lax.broadcasted_iota(jnp.int32, (LON, MEM * GL), 1), GL).astype(F32)
+    low_part = jnp.transpose((cmap[...] % GL).astype(F32))
+    for r in range(HALF):
+        for s, i in enumerate(pair(r)):
+            at = (2 * r + s) * LON
+            in_lane[at:at + LON] = jnp.where(low_part[:, i:i + 1] == low_lane, 1.0, 0.0).astype(BF16)
     loads["diff"].wait()
 
     def widen_diff(value, i):
@@ -232,8 +253,7 @@
     repeat_lane = lax.broadcasted_iota(jnp.int32, (MEM, WIDTH), 1) // GJ
     repeat = jnp.where(repeat_row == repeat_lane, 1.0, 0.0).astype(BF16)
 
-    for d in range(1, tm_count):
-        spread(d).wait_recv()
+    all_here(0, gathered.at[others])
     weights = jnp.concatenate([gathered[p] for p in range(tm_count)], axis=1)
     def pick(r):
         found = []
@@ -382,16 +402,16 @@
             known_u.add((H, r))
             final(r, value)
 
-    level_row = lax.broadcasted_iota(jnp.int32, (MEM * LEV, 2 * MEM), 0) // LEV
-    level_lane = lax.broadcasted_iota(jnp.int32, (MEM * LEV, 2 * MEM), 1) % MEM
+    level_row = lax.broadcasted_iota(jnp.int32, (MEM * LEV, MEM), 0) // LEV
+    level_lane = lax.broadcasted_iota(jnp.int32, (MEM * LEV, MEM), 1)
     own = jnp.where(level_row == level_lane, 1.0, 0.0).astype(BF16)
-    is_high = lax.broadcasted_iota(jnp.int32, (2 * LON, 2 * MEM), 1) < MEM
-    cut = max(HALF // 2, 1)
-    parts = [list(range(0, cut)), list(range(cut, HALF))]
+    copy_row = lax.broadcasted_iota(jnp.int32, (MEM, MEM * GL), 0)
+    copy_lane = lax.broadcasted_iota(jnp.int32, (MEM, MEM * GL), 1) // GL
+    copies = jnp.where(copy_row == copy_lane, 1.0, 0.0).astype(BF16)
     totals = []
 
     def final(r, value):
-        got(has_prev, *rows_of(end_on, r))
+        got(has_prev, (prev_base + r, end_prev.at[pl.ds(0, 2)]))
         terms = []
         for s, i in enumerate(pair(r)):
             total = prec[i].astype(F32) * (start[i] - end_prev[i].astype(F32)) + value[s]
@@ -399,17 +419,12 @@
             rounded = total.astype(BF16)
             terms.append(jnp.concatenate([pert[k, i] * rounded for k in range(MEM)], axis=1))
         summed = jnp.concatenate([jnp.dot(t, own, preferred_element_type=F32) for t in terms], axis=0)
-        high = summed.astype(BF16).astype(F32)
+        spread_cells = jnp.dot(summed.astype(BF16), copies, preferred_element_type=F32).astype(BF16)
         at = 2 * r * LON
-        contrib[at:at + 2 * LON] = jnp.where(is_high, high, summed - high).astype(BF16)
-        for part in parts:
-            if r in part and all((H, q) in known_u for q in part):
-                at, until = 2 * part[0] * LON, 2 * (part[-1] + 1) * LON
-                share = jnp.dot(onehot[:, at:until], contrib[at:until], preferred_element_type=F32)
-                if totals:
-                    share = share + sums_buf[...]
-                sums_buf[...] = share
-                totals.append(part)
+        placed_terms = spread_cells * in_lane[at:at + 2 * LON]
+        share = jnp.dot(in_group[:, at:at + 2 * LON], placed_terms, preferred_element_type=F32)
+        sums_buf[...] = share + sums_buf[...] if totals else share
+        totals.append(r)
 
     def leading(goals):
         need_c, need_s, stack = set(), set(), []
@@ -455,8 +470,8 @@
             value.append(misfit - prec_next[i].astype(F32) * (start_next[i].astype(F32) - end))
         have_u(0, r, value)
 
-    got(has_down, diff_up)
-    got(has_up, diff_down)
+    got(has_down, (2, diff_halo.at[1]))
+    got(has_up, (3, diff_halo.at[0]))
     for q in range(1, D + 1):
         widen_diff(diff_halo[0, D - q], D - q)
         widen_diff(diff_halo[1, q - 1], R - 1 + D + q)
@@ -464,16 +479,14 @@
     urgent = {(supplied(k)[0], supplied(k)[1] - 1) for k in range(H)}
 
     def seed_and_send(r):
-        got(has_next, *rows_of(prec_back, r), *rows_of(start_back, r))
+        got(has_next, (next_base + r, prec_next.at[pl.ds(0, 4)]))
         seed(r)
         adjoint(urgent)
 
-    split = max(H - 2, 0)
     seeded = []
-    for some in [range(split)] + [range(k, k + 1) for k in range(split, H)]:
-        for k in some:
-            got(has_down, fwd_up[k])
-            got(has_up, fwd_down[k])
+    for some in early_groups:
+        got(has_down, (fwd_sem[some[0]], fwd_recv.at[1, pl.ds(0, len(some))]))
+        got(has_up, (fwd_sem[some[0]] + 1, fwd_recv.at[0, pl.ds(0, len(some))]))
         for k in some:
             n, depth = supplied(k)
             fwd_row(n, -depth, [fwd_recv[s, k].astype(F32) for s in range(2)], send=False)
@@ -487,12 +500,9 @@
             seed_and_send(r)
     adjoint()
 
-    order = [1, 0] + list(range(2, H)) if H > 1 else [0]
-    for first in range(0, H, 2):
-        some = order[first:first + 2]
-        for k in some:
-            got(has_down, adj_up[k])
-            got(has_up, adj_down[k])
+    for some in late_groups:
+        got(has_down, (adj_sem[some[0]], adj_recv.at[1, pl.ds(0, len(some))]))
+        got(has_up, (adj_sem[some[0]] + 1, adj_recv.at[0, pl.ds(0, len(some))]))
         for k in some:
             m, depth = supplied(k)
             value = [adj_recv[s, k].astype(F32) for s in range(2)]
@@ -504,26 +514,33 @@
                 known_w.add((m, -depth))
         adjoint()
 
-    sums = jnp.transpose(sums_buf[...])
-    sums = sums[0:MEM] + sums[MEM:2 * MEM]
     for p in range(tm_count):
-        term_send[p] = sums[:, p * CW:(p + 1) * CW]
+        term_send[p] = sums_buf[p * HB:(p + 1) * HB]
     for d in range(1, tm_count):
         term(d).start()
-    result = gathered[me_t] + term_send[me_t]
-    for d in range(1, tm_count):
-        term(d).wait_recv()
+    result = term_send[me_t]
+    all_here(1, term_recv.at[others])
     for d in range(1, tm_count):
         result = result + term_recv[lax.rem(me_t + d, tm_count)]
-    gw_ref[:, 0, :] = result
-
-    for d in range(1, tm_count):
-        spread(d).wait_send()
-        term(d).wait_send()
-    sent(has_up, diff_up, *fwd_up, *adj_up)
-    sent(has_down, diff_down, *fwd_down, *adj_down)
-    sent(has_prev, *prec_back, *start_back)
-    sent(has_next, *end_on)
+    out_row = lax.broadcasted_iota(jnp.int32, (MEM, LANES), 0)
+    out_lane = lax.broadcasted_iota(jnp.int32, (MEM, LANES), 1)
+    owned = jnp.zeros((MEM, LANES), F32)
+    for b in range(0, MEM * GL, LANES):
+        where_from = out_row * GL + lax.rem(out_lane, GL) - b
+        inside = (where_from >= 0) & (where_from < LANES)
+        where_from = jnp.clip(where_from, 0, LANES - 1)
+        for h in range(HB):
+            source = jnp.broadcast_to(result[h:h + 1, b:b + LANES], (MEM, LANES))
+            taken = jnp.take_along_axis(source, where_from, axis=1)
+            owned = jnp.where(inside & (out_lane // GL == h), taken, owned)
+    gw_ref[:, 0, :] = owned[:, 0:CW] + gathered[me_t]
+
+    all_sent(0, gathered.at[others])
+    all_sent(1, term_send.at[others])
+    sent(has_up, (2, diff_halo.at[0]), (7, fwd_send.at[0]), (9, adj_send.at[0]))
+    sent(has_down, (3, diff_halo.at[1]), (8, fwd_send.at[1]), (10, adj_send.at[1]))
+    sent(has_prev, (4, prec_next), (5, start_next))
+    sent(has_next, (6, end_prev))
 
 
 def deliver(grad, owned, grad_h, gw_h, sem):
@@ -547,6 +564,7 @@
         D = max(H // 2, 1)
         DS = max(supplied(k)[1] for k in range(H))
         C = CW * tm_count
+        GL = min(WIDTH // MEM, CW)
         field = lambda rows, kind: pltpu.VMEM((rows, LON, LEV), kind)
         padded = pltpu.VMEM((H, R + 2 * DS, LON + 2 * EDGE, LEV), F32)
         halo = pltpu.VMEM((2, H, LON, LEV), BF16)
@@ -564,19 +582,19 @@
             pltpu.VMEM((H, LEV, LEV), BF16),
             pltpu.VMEM((H, LEV, LEV), BF16),
             pltpu.VMEM((1, R * LON), jnp.int32),
-            pltpu.VMEM((C, 2 * MEM), F32),
-            pltpu.VMEM((C, R * LON), BF16),
+            pltpu.VMEM((C // GL, MEM * GL), F32),
+            pltpu.VMEM((C // GL, R * LON), BF16),
+            pltpu.VMEM((R * LON, MEM * GL), BF16),
             field(R, F32), field(R, BF16), padded, padded,
             field(R + 2 * D, F32), field(R + 2 * D, F32),
             field(R, F32), field(R, BF16), field(R, BF16), field(R, BF16), field(R, BF16),
             halo, halo, halo, halo,
-            pltpu.VMEM((R * LON, 2 * MEM), BF16),
-            pltpu.VMEM((tm_count, MEM, CW), F32),
-            pltpu.VMEM((tm_count, MEM, CW), F32),
+            pltpu.VMEM((tm_count, CW // GL, MEM * GL), F32),
+            pltpu.VMEM((tm_count, CW // GL, MEM * GL), F32),
             pltpu.SemaphoreType.DMA((10,)),
-            pltpu.SemaphoreType.DMA((2 + 3 * R + 4 * H,)),
-            pltpu.SemaphoreType.DMA((2 + 3 * R + 4 * H,)),
-        ] + [pltpu.SemaphoreType.DMA((tm_count,))] * 4
+            pltpu.SemaphoreType.DMA((11,)),
+            pltpu.SemaphoreType.DMA((4 + 2 * min(H, 3) + 2 * (-(-H // 2)) + R,)),
+        ]
 
         def run(*refs):
             kernel(tm_count, lat_count, (H, R, LON, LEV, MEM, CW), *refs)

time: 30.9 us -> 29.1 us (0.942)
  Pallas kernels: 29.5 us -> 27.6 us
    pallas_call x1, Pallas kernels: 28.6 us -> 26.7 us  [body(): pl.pallas_call(run, out_shape=(pltpu.VMEM(incr.shape, F32), pltpu.VMEM((M...]
where the time goes in v3:
time: 29.1 us; the launch traced here: 28.9 us
  Pallas kernels  27.6 us (95%)
  between operations  1.29 us (4%)
    pallas_call x1, Pallas kernels, body(): pl.pallas_call(run, out_shape=(pltpu.VMEM(incr.shape, F32), pltpu.VMEM((M...  26.7 us
    pallas_call x1, Pallas kernels, body(): pl.pallas_call(deliver, out_shape=(jax.ShapeDtypeStruct(incr.shape, F32),...  0.9 us

profile of v3, /device:TPU:0, one launch (start us, length us, event | category | flops | bytes accessed | tf_op | source)
XLA Modules:
  0.0 28.9 jit_solution(15691423027649862778)
XLA Ops:
  1.3 26.7 %shard_map.122 = (f32[1,8,192,128]{3,2,1,0:T(8,128)S(1)}, f32[8,1,128]{2,1,0:T(1,128)S(1)}) custom-call(s32[1]{0:T(128)S(6)} %copy.13.refs_0_, f32[1,8,192,128]{3,2,1,0:T(8,128)} %refs_1_.1, bf16[8,1,8,192,128]{4,3,2,1,0:T(8,128)(2,1)} %refs_2_.1, f32[8,1,128]{2,1,0:T(1,128)} %refs_3_.1, s32[8,192]{1,0:T(8,128)} %refs_4_.1, ...), custom_call_target="tpu_custom_call" | custom-call | tf_op jit(solution)/shard_map/pallas_call | solution.py:606
  28.0 0.9 %shard_map.123 = (f32[1,8,192,128]{3,2,1,0:T(8,128)}, f32[8,1,128]{2,1,0:T(1,128)}) custom-call(f32[1,8,192,128]{3,2,1,0:T(8,128)S(1)} %get-tuple-element.4.grad, f32[8,1,128]{2,1,0:T(1,128)S(1)} %get-tuple-element.5.owned), custom_call_target="tpu_custom_call" | custom-call | tf_op jit(solution)/shard_map/pallas_call | solution.py:621

commit v4 on v3

--- a/solution.py
+++ b/solution.py
@@ -35,6 +35,7 @@
     me_t, me_l = lax.axis_index("tm"), lax.axis_index("lat")
     has_up, has_down = me_l > 0, me_l < lat_count - 1
     has_prev, has_next = me_t > 0, me_t < tm_count - 1
+    first_core, second_core = lax.rem(me_t, 2) == 0, lax.rem(me_t, 2) == 1
 
     def pair(r):
         return (r, R - 1 - r)
@@ -249,10 +250,6 @@
         return found
 
     placed = [places(r) for r in range(HALF)]
-    repeat_row = lax.broadcasted_iota(jnp.int32, (MEM, WIDTH), 0)
-    repeat_lane = lax.broadcasted_iota(jnp.int32, (MEM, WIDTH), 1) // GJ
-    repeat = jnp.where(repeat_row == repeat_lane, 1.0, 0.0).astype(BF16)
-
     all_here(0, gathered.at[others])
     weights = jnp.concatenate([gathered[p] for p in range(tm_count)], axis=1)
     def pick(r):
@@ -262,12 +259,12 @@
             for c in range(C // LANES):
                 taken = jnp.take_along_axis(weights[:, c * LANES:(c + 1) * LANES], inside, axis=1)
                 value = jnp.where(block == c, taken, value)
-            found.append(jnp.transpose(value))
-        return jnp.concatenate(found, axis=0).astype(BF16)
+            wide = jnp.broadcast_to(value[:, None, :], (MEM, GJ, LANES)).reshape(WIDTH, LANES)
+            found.append(jnp.transpose(wide))
+        return jnp.concatenate(found, axis=0)
 
     def begin(r):
-        cells = pick(r)
-        picked = jnp.dot(cells, repeat, preferred_element_type=F32)
+        picked = pick(r)
         value = []
         for s, i in enumerate(pair(r)):
             pieces = []
@@ -300,7 +297,6 @@
             for s, i in enumerate(pair(r)):
                 end_buf[i] = result[s]
                 end_bf[i] = result[s].astype(BF16)
-            go(has_next, *rows_of(end_on, r))
 
     def fold(r):
         return R - 1 - r if r >= HALF else r
@@ -366,8 +362,12 @@
     def adj_send_row(k, value):
         for s in range(2):
             adj_send[s, k] = value[s].astype(BF16)
-        go(has_up, adj_up[k])
-        go(has_down, adj_down[k])
+        if k in (2, 3):
+            go(jnp.logical_and(has_up, first_core), adj_up[k])
+            go(jnp.logical_and(has_down, first_core), adj_down[k])
+        else:
+            go(has_up, adj_up[k])
+            go(has_down, adj_down[k])
 
     def have_u(m, r, value):
         for s, i in enumerate(pair(r)):
@@ -496,9 +496,16 @@
             seed_and_send(1)
             seeded.append(1)
     for r in range(HALF):
+        if r == HALF - 1:
+            for q in reversed(range(HALF)):
+                go(has_next, *rows_of(end_on, q))
         if r not in seeded:
             seed_and_send(r)
     adjoint()
+    for k in range(H):
+        if k in (2, 3):
+            go(jnp.logical_and(has_up, second_core), adj_up[k])
+            go(jnp.logical_and(has_down, second_core), adj_down[k])
 
     for some in late_groups:
         got(has_down, (adj_sem[some[0]], adj_recv.at[1, pl.ds(0, len(some))]))

time: 29.1 us -> 28.5 us (0.979)
  Pallas kernels: 27.6 us -> 27 us
    pallas_call x1, Pallas kernels: 26.7 us -> 26.1 us  [body(): pl.pallas_call(run, out_shape=(pltpu.VMEM(incr.shape, F32), pltpu.VMEM((M...]
where the time goes in v4:
time: 28.5 us; the launch traced here: 28.3 us
  Pallas kernels  27 us (95%)
  between operations  1.29 us (5%)
    pallas_call x1, Pallas kernels, body(): pl.pallas_call(run, out_shape=(pltpu.VMEM(incr.shape, F32), pltpu.VMEM((M...  26.1 us
    pallas_call x1, Pallas kernels, body(): pl.pallas_call(deliver, out_shape=(jax.ShapeDtypeStruct(incr.shape, F32),...  0.9 us

profile of v4, /device:TPU:0, one launch (start us, length us, event | category | flops | bytes accessed | tf_op | source)
XLA Modules:
  0.0 28.3 jit_solution(8638831844197728168)
XLA Ops:
  1.3 26.1 %shard_map.122 = (f32[1,8,192,128]{3,2,1,0:T(8,128)S(1)}, f32[8,1,128]{2,1,0:T(1,128)S(1)}) custom-call(s32[1]{0:T(128)S(6)} %copy.13.refs_0_, f32[1,8,192,128]{3,2,1,0:T(8,128)} %refs_1_.1, bf16[8,1,8,192,128]{4,3,2,1,0:T(8,128)(2,1)} %refs_2_.1, f32[8,1,128]{2,1,0:T(1,128)} %refs_3_.1, s32[8,192]{1,0:T(8,128)} %refs_4_.1, ...), custom_call_target="tpu_custom_call" | custom-call | tf_op jit(solution)/shard_map/pallas_call | solution.py:613
  27.4 0.9 %shard_map.123 = (f32[1,8,192,128]{3,2,1,0:T(8,128)}, f32[8,1,128]{2,1,0:T(1,128)}) custom-call(f32[1,8,192,128]{3,2,1,0:T(8,128)S(1)} %get-tuple-element.4.grad, f32[8,1,128]{2,1,0:T(1,128)S(1)} %get-tuple-element.5.owned), custom_call_target="tpu_custom_call" | custom-call | tf_op jit(solution)/shard_map/pallas_call | solution.py:628

commit v5 on v4

--- a/solution.py
+++ b/solution.py
@@ -234,8 +234,12 @@
                 if n > 0:
                     for s in range(2):
                         fwd_send[s, k] = value[s].astype(BF16)
-                go(has_up, fwd_up[k])
-                go(has_down, fwd_down[k])
+                if k in (1, 2, 3):
+                    go(jnp.logical_and(has_up, first_core), fwd_up[k])
+                    go(jnp.logical_and(has_down, first_core), fwd_down[k])
+                else:
+                    go(has_up, fwd_up[k])
+                    go(has_down, fwd_down[k])
 
     row = lax.broadcasted_iota(jnp.int32, (GJ, WIDTH), 0)
     lane = lax.broadcasted_iota(jnp.int32, (GJ, WIDTH), 1)
@@ -335,6 +339,11 @@
             for q in late:
                 go(has_prev, *rows_of(prec_back, q))
         forward()
+
+    for k in range(H):
+        if k in (1, 2, 3):
+            go(jnp.logical_and(has_up, second_core), fwd_up[k])
+            go(jnp.logical_and(has_down, second_core), fwd_down[k])
 
     wanted_u, wanted_w = set(), set()
 

time: 28.5 us -> 28.3 us (level)
  no operation moved by 1% of the time
where the time goes in v5:
time: 28.3 us; the launch traced here: 28.1 us
  Pallas kernels  26.8 us (95%)
  between operations  1.29 us (5%)
    pallas_call x1, Pallas kernels, body(): pl.pallas_call(run, out_shape=(pltpu.VMEM(incr.shape, F32), pltpu.VMEM((M...  25.9 us
    pallas_call x1, Pallas kernels, body(): pl.pallas_call(deliver, out_shape=(jax.ShapeDtypeStruct(incr.shape, F32),...  0.9 us

profile of v5, /device:TPU:0, one launch (start us, length us, event | category | flops | bytes accessed | tf_op | source)
XLA Modules:
  0.0 28.1 jit_solution(14037066568313686638)
XLA Ops:
  1.3 25.9 %shard_map.122 = (f32[1,8,192,128]{3,2,1,0:T(8,128)S(1)}, f32[8,1,128]{2,1,0:T(1,128)S(1)}) custom-call(s32[1]{0:T(128)S(6)} %copy.13.refs_0_, f32[1,8,192,128]{3,2,1,0:T(8,128)} %refs_1_.1, bf16[8,1,8,192,128]{4,3,2,1,0:T(8,128)(2,1)} %refs_2_.1, f32[8,1,128]{2,1,0:T(1,128)} %refs_3_.1, s32[8,192]{1,0:T(8,128)} %refs_4_.1, ...), custom_call_target="tpu_custom_call" | custom-call | tf_op jit(solution)/shard_map/pallas_call | solution.py:622
  27.2 0.9 %shard_map.123 = (f32[1,8,192,128]{3,2,1,0:T(8,128)}, f32[8,1,128]{2,1,0:T(1,128)}) custom-call(f32[1,8,192,128]{3,2,1,0:T(8,128)S(1)} %get-tuple-element.4.grad, f32[8,1,128]{2,1,0:T(1,128)S(1)} %get-tuple-element.5.owned), custom_call_target="tpu_custom_call" | custom-call | tf_op jit(solution)/shard_map/pallas_call | solution.py:637

commit v6 on v5

--- a/solution.py
+++ b/solution.py
@@ -291,7 +291,7 @@
 
     def step(n, r):
         here = [s_buf[n, i + DS, EDGE:EDGE + LON] for i in pair(r)]
-        smoothed = [e_buf[i + D] * here[s] + d_buf[i + D] * around(s_buf, n, i + DS) for s, i in enumerate(pair(r))]
+        smoothed = [here[s] + d_buf[i + D] * (around(s_buf, n, i + DS) - 4.0 * here[s]) for s, i in enumerate(pair(r))]
         result = modes(smoothed, both[n])
         if n > 0:
             result = [jnp.where(n < step_count, a, b) for a, b in zip(result, here)]

time: 28.3 us -> 28.3 us (level)
  no operation moved by 1% of the time
where the time goes in v6:
time: 28.3 us; the launch traced here: 28.1 us
  Pallas kernels  26.9 us (95%)
  between operations  1.29 us (5%)
    pallas_call x1, Pallas kernels, body(): pl.pallas_call(run, out_shape=(pltpu.VMEM(incr.shape, F32), pltpu.VMEM((M...  26 us
    pallas_call x1, Pallas kernels, body(): pl.pallas_call(deliver, out_shape=(jax.ShapeDtypeStruct(incr.shape, F32),...  0.9 us

profile of v6, /device:TPU:0, one launch (start us, length us, event | category | flops | bytes accessed | tf_op | source)
XLA Modules:
  0.0 28.1 jit_solution(8154899034771727902)
XLA Ops:
  1.3 26.0 %shard_map.122 = (f32[1,8,192,128]{3,2,1,0:T(8,128)S(1)}, f32[8,1,128]{2,1,0:T(1,128)S(1)}) custom-call(s32[1]{0:T(128)S(6)} %copy.13.refs_0_, f32[1,8,192,128]{3,2,1,0:T(8,128)} %refs_1_.1, bf16[8,1,8,192,128]{4,3,2,1,0:T(8,128)(2,1)} %refs_2_.1, f32[8,1,128]{2,1,0:T(1,128)} %refs_3_.1, s32[8,192]{1,0:T(8,128)} %refs_4_.1, ...), custom_call_target="tpu_custom_call" | custom-call | tf_op jit(solution)/shard_map/pallas_call | solution.py:622
  27.2 0.9 %shard_map.123 = (f32[1,8,192,128]{3,2,1,0:T(8,128)}, f32[8,1,128]{2,1,0:T(1,128)}) custom-call(f32[1,8,192,128]{3,2,1,0:T(8,128)S(1)} %get-tuple-element.4.grad, f32[8,1,128]{2,1,0:T(1,128)S(1)} %get-tuple-element.5.owned), custom_call_target="tpu_custom_call" | custom-call | tf_op jit(solution)/shard_map/pallas_call | solution.py:637
